TPU v7x, 128 devices: a whole 4x4x4 slice. The times are simulated.
128 devices in a mesh: seq: 16 (over z, x), req: 8 (over y, core).
Axes of the slice: x: 4, y: 4, z: 4, core: 2. Of those that a mesh axis runs over, the one named last changes fastest.
Arguments:
- given_token_index: int32 [128], replicated, may hold values from 0 to 31999
- hidden: bfloat16 [128, 3584], P('req'), may hold values from -6 to 6
- token_embedding_table: bfloat16 [32000, 3584], P(('seq', 'req')), may hold values from -6 to 6
- attention_norm_gain: bfloat16 [7168], replicated, may hold values from 0.099609375 to 1.8984375
- query_key_value_weight: bfloat16 [7168, 10752], P('req', 'seq'), may hold values from -0.0625 to 0.0625
- rotated_key_cache: bfloat16 [96, 8, 128, 3584], P('seq', 'req'), may hold values from -240 to 240
- cached_value_pages: bfloat16 [96, 8, 128, 3584], P('seq', 'req'), may hold values from -6 to 6
- lengths: int32 [32], P('req'), may hold values from 1 to 6144, as said below
- request_page_slots: int32 [32, 48], P('req'), may hold values from 0 to 95, as said below
- attention_output_weight: bfloat16 [3584, 7168], P('seq'), may hold values from -0.375 to 0.375
- feedforward_norm_gain: bfloat16 [7168], replicated, may hold values from 0.099609375 to 1.8984375
- gate_weight: bfloat16 [7168, 14336], P('req', 'seq'), may hold values from -0.0625 to 0.0625
- up_weight: bfloat16 [7168, 14336], P('req', 'seq'), may hold values from -0.0625 to 0.0625
- adapter_down_map: bfloat16 [7168, 128], P('req'), may hold values from -0.0625 to 0.0625
- adapter_gate_map: bfloat16 [128, 14336], P(None, 'seq'), may hold values from -0.5 to 0.5
- adapter_up_map: bfloat16 [128, 14336], P(None, 'seq'), may hold values from -0.5 to 0.5
- down_weight: bfloat16 [14336, 7168], P('seq', 'req'), may hold values from -0.046875 to 0.046875
Outputs:
- block_out: bfloat16 [128, 7168], P('seq', 'req')
Inputs may be any that keep to these rules, and one draw needn't show every extreme that they name: `lengths`: in each group of 4 requests exactly one has 6144 tokens, and the pages of a group's requests number at most 96 together. `request_page_slots`: entry p of request i names a slot of its group, 0 to 95; the entries with p * 128 below lengths[i] are distinct within a group, the others name any slot. Slot g of a group lies on the seq index g // 6, at place g % 6.
All inputs are finite; a program needn't handle non-finite values.
Results may differ from a plain program's by a relative error of at most 0.028.
The roundings to bfloat16 on the way count: a program that leaves them out, or rounds other values in their place, can miss the bound.
Values may be sent and summed in bfloat16 or wider, within the bound.
A program may use at most 128 MiB of HBM per device.

v0:
```python
import math
import jax
import jax.numpy as jnp
from jax import lax
from jax.sharding import PartitionSpec as P

HEADS = 16
HD = 224
NEGATIVE = -1e30
EPSILON = 1e-05
ROTARY_BASE = 10000.0


def merged_2(array, axis, combine):
    everything = jax.tree.map(lambda part: lax.all_gather(part, axis), array)
    first = jax.tree.map(lambda part: part[0], everything)

    def hop(k, so_far):
        return combine(so_far, jax.tree.map(lambda part: part[k], everything))

    return lax.fori_loop(1, lax.axis_size(axis), hop, first)


def rms_norm(matrix, gain_vec):
    widened = matrix.astype(jnp.float32)
    factor = lax.rsqrt(jnp.mean(widened * widened, axis=-1, keepdims=True) + EPSILON)
    return (widened * factor * gain_vec.astype(jnp.float32)).astype(jnp.bfloat16)


def rotate(vectors, positions):
    half_dim = vectors.shape[-1] // 2
    frequency = ROTARY_BASE ** (-2.0 * jnp.arange(half_dim, dtype=jnp.float32) / vectors.shape[-1])
    angles = positions.astype(jnp.float32)[..., None, None] * frequency
    cosine = jnp.cos(angles)
    sine_part = jnp.sin(angles)
    front_half = vectors[..., :half_dim]
    back_half = vectors[..., half_dim:]
    return jnp.concatenate(
        [front_half * cosine - back_half * sine_part, back_half * cosine + front_half * sine_part],
        axis=-1,
    )


def softmax_join(earlier, later):
    first_max, first_sum, first_out = earlier
    second_max, second_sum, second_out = later
    overall = jnp.maximum(first_max, second_max)
    first_factor = jnp.exp(first_max - overall)
    second_factor = jnp.exp(second_max - overall)
    return (
        overall,
        first_sum * first_factor + second_sum * second_factor,
        first_out * first_factor[..., None] + second_out * second_factor[..., None],
    )


def body(
    given_token_index,
    hidden,
    token_embedding_table,
    attention_norm_gain,
    query_key_value_weight,
    rotated_key_cache,
    cached_value_pages,
    lengths,
    request_page_slots,
    attention_output_weight,
    feedforward_norm_gain,
    gate_weight,
    up_weight,
    adapter_down_map,
    adapter_gate_map,
    adapter_up_map,
    down_weight,
):
    seq_devices = lax.axis_size("seq")
    req_devices = lax.axis_size("req")
    seq_index = lax.axis_index("seq")
    req_index = lax.axis_index("req")
    group_rows = hidden.shape[0]
    requests = lengths.shape[0]
    steps_each = group_rows // requests
    vocab_rows = token_embedding_table.shape[0]
    first_id = (seq_index * req_devices + req_index) * vocab_rows
    local_ids = given_token_index - first_id
    present = (local_ids >= 0) & (local_ids < vocab_rows)
    looked = jnp.take(token_embedding_table, jnp.clip(local_ids, 0, vocab_rows - 1), axis=0).astype(
        jnp.float32
    )
    looked = jnp.where(present[:, None], looked, 0.0)
    everywhere = lax.psum(looked, ("seq", "req"))
    embedded = lax.dynamic_slice_in_dim(everywhere, req_index * group_rows, group_rows, 0)
    joined = jnp.concatenate([hidden, embedded.astype(jnp.bfloat16)], axis=1)
    normed = rms_norm(joined, attention_norm_gain)
    spread = lax.all_to_all(normed, "req", split_axis=1, concat_axis=0, tiled=True)
    block_rows = spread
    qkv_part = lax.psum_scatter(
        jnp.dot(block_rows, query_key_value_weight, preferred_element_type=jnp.float32),
        "req",
        scatter_dimension=0,
        tiled=True,
    )
    projected = lax.all_gather(qkv_part.astype(jnp.bfloat16), "seq", axis=1, tiled=True)
    head_cols = HEADS * HD
    queries = projected[:, :head_cols].reshape(requests, steps_each, HEADS, HD)
    new_keys = projected[:, head_cols : 2 * head_cols].reshape(requests, steps_each, HEADS, HD)
    new_values = projected[:, 2 * head_cols :].reshape(requests, steps_each, HEADS, HD)
    positions = lengths[:, None] + jnp.arange(steps_each, dtype=jnp.int32)[None, :]
    queries = rotate(queries.astype(jnp.float32), positions).astype(jnp.bfloat16)
    new_keys = rotate(new_keys.astype(jnp.float32), positions).astype(jnp.bfloat16)
    slots = rotated_key_cache.shape[0]
    page_len = rotated_key_cache.shape[2]
    cache_k = rotated_key_cache.reshape(slots * page_len, HEADS, HD)
    cache_v = cached_value_pages.reshape(slots * page_len, HEADS, HD)
    slot_ids = seq_index * slots + jnp.arange(slots, dtype=jnp.int32)
    page_ids = jnp.arange(request_page_slots.shape[1], dtype=jnp.int32)
    is_live = page_ids[None, :] < ((lengths + page_len - 1) // page_len)[:, None]
    matches = (request_page_slots[:, :, None] == slot_ids[None, None, :]) & is_live[:, :, None]
    is_owned = jnp.any(matches, axis=1)
    page_of = jnp.sum(jnp.where(matches, page_ids[None, :, None], 0), axis=1)
    token_pos = (
        page_of[:, :, None] * page_len + jnp.arange(page_len, dtype=jnp.int32)[None, None, :]
    )
    is_valid = (is_owned[:, :, None] & (token_pos < lengths[:, None, None])).reshape(
        requests, slots * page_len
    )
    score_scale = 1.0 / math.sqrt(HD)
    scores = (
        jnp.einsum("rthd,khd->rthk", queries, cache_k, preferred_element_type=jnp.float32)
        * score_scale
    )
    mask_b = is_valid[:, None, None, :]
    local_max = jnp.max(jnp.where(mask_b, scores, NEGATIVE), axis=-1)
    weights = jnp.where(mask_b, jnp.exp(scores - local_max[..., None]), 0.0)
    local_sum = jnp.sum(weights, axis=-1)
    local_out = jnp.einsum(
        "rthk,khd->rthd", weights.astype(jnp.bfloat16), cache_v, preferred_element_type=jnp.float32
    )
    fresh_scores = (
        jnp.einsum("rthd,rshd->rths", queries, new_keys, preferred_element_type=jnp.float32)
        * score_scale
    )
    causal = jnp.arange(steps_each)[:, None] >= jnp.arange(steps_each)[None, :]
    fresh_mask = causal[None, :, None, :]
    fresh_max = jnp.max(jnp.where(fresh_mask, fresh_scores, NEGATIVE), axis=-1)
    fresh_w = jnp.where(fresh_mask, jnp.exp(fresh_scores - fresh_max[..., None]), 0.0)
    fresh_sum = jnp.sum(fresh_w, axis=-1)
    fresh_out = jnp.einsum(
        "rths,rshd->rthd",
        fresh_w.astype(jnp.bfloat16),
        new_values,
        preferred_element_type=jnp.float32,
    )
    own_heads = HEADS // seq_devices
    first_head = seq_index * own_heads

    def own_slice(member):
        return lax.dynamic_slice_in_dim(member, first_head, own_heads, 2)

    fresh_part = (own_slice(fresh_max), own_slice(fresh_sum), own_slice(fresh_out))
    merged = merged_2((local_max, local_sum, local_out), "seq", softmax_join)
    combined = softmax_join(tuple((own_slice(member) for member in merged)), fresh_part)
    attention = (
        (combined[2] / combined[1][..., None])
        .astype(jnp.bfloat16)
        .reshape(group_rows, own_heads * HD)
    )
    projected_out = jnp.dot(attention, attention_output_weight, preferred_element_type=jnp.float32)
    mixed_sum = lax.psum(projected_out, "seq")
    after_attn = (joined.astype(jnp.float32) + mixed_sum).astype(jnp.bfloat16)
    second_normed_state = rms_norm(after_attn, feedforward_norm_gain)
    residual_cols, second_spread_state = (
        lax.all_to_all(after_attn, "req", split_axis=1, concat_axis=0, tiled=True),
        lax.all_to_all(second_normed_state, "req", split_axis=1, concat_axis=0, tiled=True),
    )
    gate_total, up_total, low_sum = lax.psum(
        (
            jnp.dot(second_spread_state, gate_weight, preferred_element_type=jnp.float32),
            jnp.dot(second_spread_state, up_weight, preferred_element_type=jnp.float32),
            jnp.dot(second_spread_state, adapter_down_map, preferred_element_type=jnp.float32),
        ),
        "req",
    )
    adapter_hidden = low_sum.astype(jnp.bfloat16)
    gate_preactivation = gate_total + jnp.dot(
        adapter_hidden, adapter_gate_map, preferred_element_type=jnp.float32
    )
    up_projection_part = up_total + jnp.dot(
        adapter_hidden, adapter_up_map, preferred_element_type=jnp.float32
    )
    inner_act = (jax.nn.silu(gate_preactivation) * up_projection_part).astype(jnp.bfloat16)
    out_rows = residual_cols.shape[0] // seq_devices
    block_rows = inner_act
    down_sum = lax.psum_scatter(
        jnp.dot(block_rows, down_weight, preferred_element_type=jnp.float32),
        "seq",
        scatter_dimension=0,
        tiled=True,
    )
    residual_rows = lax.dynamic_slice_in_dim(residual_cols, seq_index * out_rows, out_rows, 0)
    return (residual_rows.astype(jnp.float32) + down_sum).astype(jnp.bfloat16)


def solution(mesh):
    placed = (
        P(),
        P("req", None),
        P(("seq", "req"), None),
        P(),
        P("req", "seq"),
        P("seq", "req", None, None),
        P("seq", "req", None, None),
        P("req"),
        P("req", None),
        P("seq", None),
        P(),
        P("req", "seq"),
        P("req", "seq"),
        P("req", None),
        P(None, "seq"),
        P(None, "seq"),
        P("seq", "req"),
    )
    return jax.shard_map(
        body, mesh=mesh, in_specs=placed, out_specs=P("seq", "req"), check_vma=False
    )
```

profile of v0, /device:TPU:0, one launch (start us, length us, event | category | flops | bytes accessed | tf_op | source)
XLA Modules:
  0.0 529.0 jit_solution(585776612457046075)
XLA Ops:
  7.4 4.9 gather_fusion
  12.2 2.8 convert_select_fusion
  15.0 74.1 %all-reduce.12 = bf16[128,3584]{1,0:T(8,128)(2,1)} all-reduce(f32[128,3584]{1,0:T(8,128)} %convert_select_fusion), channel_id=1, replica_groups=mesh['seq'=16,'req'=8] {'seq','req'}, use_global_device_ids=true, to_apply=%region_0.1 | all-reduce | flops 458752 | bytes 2752512 | tf_op jit(solution)/shard_map/psum | solution.py:91
  92.9 1.0 multiply_convert_fusion
  94.6 3.9 all-to-all-start
  100.2 1.5 fusion.55
  102.9 1.3 copy.111
  104.2 1.3 broadcast_bitcast_fusion.1
  105.4 1.3 add_convert_fusion.2
  106.7 2.6 fusion.67
  110.2 13.1 %reshape.185 = bf16[768,16,224]{2,1,0:T(8,128)(2,1)} reshape(bf16[6,1,128,3584]{3,2,1,0:T(8,128)(2,1)} %param.24) | data formatting | bytes 11010048 | tf_op jit(solution)/shard_map/reshape | solution.py:113
  123.3 13.2 %reshape.186 = bf16[768,16,224]{2,1,0:T(8,128)(2,1)} reshape(bf16[6,1,128,3584]{3,2,1,0:T(8,128)(2,1)} %param.25) | data formatting | bytes 11010048 | tf_op jit(solution)/shard_map/reshape | solution.py:114
  138.0 1.1 reduce-scatter.2.cloned.1.call-done
  139.9 24.2 %all-gather.3 = bf16[16,672,16]{1,2,0:T(8,128)(2,1)S(1)} all-gather(bf16[1,672,16]{1,2,0:T(8,128)(2,1)S(1)} %convert_bitcast_fusion), channel_id=1, replica_groups=mesh['seq'=16,'req'=8] {'seq'}, dimensions={0}, use_global_device_ids=true | all-gather | bytes 365568 | tf_op jit(solution)/shard_map/all_gather | solution.py:103
  165.0 1.5 reshape.211
  167.4 1.1 reshape.191
  169.3 1.1 reshape.190
  170.6 1.3 subtract_convert_fusion
  171.9 6.8 %select_reduce_fusion = (f32[4,4,16]{1,0,2:T(4,128)S(1)}, f32[4,4,16,768]{3,1,0,2:T(4,128)S(1)}) fusion(pred[4,768]{1,0:T(4,128)(4,1)} %fusion.54, bf16[768,16,224,1]{2,1,0,3:T(8,128)(2,1)} %bitcast.116, bf16[4,4,16,112]{3,1,0,2:T(4,128)(2,1)S(1)} %get-tuple-element.268, bf16[4,4,16,112]{3,1,0,2:T(4,128)(2,1)S(1)} %get-tuple-element.269), kind=kOutput, calls=%fused_computation.25 | convolution fusion | flops 88899328 | bytes 6410240 | tf_op jit(solution)/shard_map/rthd,khd->rthk/dot_general | solution.py:129
  179.7 4.6 fusion.16
  185.6 2.3 fusion.21
  188.7 22.9 %all-gather.1 = f32[64,4,16]{2,1,0:T(4,128)S(1)} all-gather(f32[4,4,16]{2,1,0:T(4,128)S(1)} %copy.119), channel_id=3, replica_groups=mesh['seq'=16,'req'=8] {'seq'}, dimensions={0}, use_global_device_ids=true | all-gather | bytes 17408 | tf_op jit(solution)/shard_map/all_gather | solution.py:15
  211.7 21.9 %all-gather = f32[64,4,16]{2,1,0:T(4,128)S(1)} all-gather(f32[4,4,16]{2,1,0:T(4,128)} %copy.118), channel_id=2, replica_groups=mesh['seq'=16,'req'=8] {'seq'}, dimensions={0}, use_global_device_ids=true | all-gather | bytes 17408 | tf_op jit(solution)/shard_map/all_gather | solution.py:15
  233.6 1.2 pad_maximum_fusion.1
  235.7 1.1 copy.129
  242.3 29.8 %while.19 = (s32[]{:T(128)}, f32[4,4,16]{2,1,0:T(4,128)S(1)}, f32[4,4,16]{2,1,0:T(4,128)S(1)}, f32[4,4,16,224]{3,2,1,0:T(8,128)S(1)}, f32[16,4,4,16]{3,2,1,0:T(4...) while((s32[]{:T(128)}, f32[4,4,16]{2,1,0:T(4,128)S(1)}, ...), condition=%wide.region_8.9_spmd, body=%wide.region_7.8_spmd.sunk | while | flops 173573 | bytes 1157271 | solution.py:21
  243.0 1.0 constant_dynamic-slice_fusion.5
  245.0 1.0 constant_dynamic-slice_fusion.5
  247.0 1.0 constant_dynamic-slice_fusion.5
  249.0 1.0 constant_dynamic-slice_fusion.5
  251.0 1.0 constant_dynamic-slice_fusion.5
  253.0 1.0 constant_dynamic-slice_fusion.5
  270.9 1.0 constant_dynamic-slice_fusion.5
  274.1 1.3 fusion.68
  275.5 81.3 %all-reduce.7.cloned.1.call-done = f32[16,7168]{1,0:T(8,128)} async-done(((f32[16,7168]{1,0:T(8,128)}), f32[16,7168]{1,0:T(8,128)}) %all-reduce.7.cloned.1.call-update) | async-done | bytes 458768 | tf_op jit(solution)/shard_map/psum | solution.py:169
  356.7 1.3 fusion.24
  358.2 11.4 %all_to_all.54 = bf16[16,8,896]{2,0,1:T(8,128)(2,1)S(1)} all-to-all(bf16[16,8,896]{2,0,1:T(8,128)(2,1)S(1)} %bitcast.125), channel_id=1, replica_groups=mesh['seq'=16,'req'=8] {'req'}, dimensions={1} | all-to-all | bytes 458752 | tf_op jit(solution)/shard_map/all_to_all | solution.py:174
  369.7 1.2 fusion.69
  370.9 1.2 fusion.71
  372.2 1.2 fusion.70
  373.4 24.2 %psum.38 = bf16[128,128]{1,0:T(8,128)(2,1)S(1)} all-reduce(f32[128,128]{1,0:T(8,128)S(1)} %fusion.70), channel_id=1, replica_groups=mesh['seq'=16,'req'=8] {'req'}, use_global_device_ids=true, to_apply=%region_14.15 | all-reduce | flops 16384 | bytes 98304 | tf_op jit(solution)/shard_map/psum | solution.py:176
  397.5 34.2 %all-reduce.11.cloned.1.call-done = (f32[128,896]{1,0:T(8,128)}, f32[128,896]{1,0:T(8,128)}) async-done(((f32[128,896]{1,0:T(8,128)}, f32[128,896]{1,0:T(8,128)}), (f32[128,896]{1,0:T(8,128)}, f32[128,896]{1,0:T(8,128)})) %all-reduce.11.cloned.1.call-update) | async-done | bytes 917520 | tf_op jit(solution)/shard_map/psum | solution.py:176
  431.8 2.1 convolution_add_fusion.1
  433.9 3.2 fusion.19
  437.9 3.4 all-to-all-start.1
  442.5 5.9 %all-to-all-done.1 = bf16[16,8,896]{2,0,1:T(8,128)(2,1)S(1)} async-done(((bf16[16,8,896]{2,0,1:T(8,128)(2,1)}), bf16[16,8,896]{2,0,1:T(8,128)(2,1)S(1)}, u32[]{:S(2)}, u32[]{:S(2)}) %all-to-all-start.1) | async-done | bytes 229408 | tf_op jit(solution)/shard_map/all_to_all | solution.py:173
  448.4 72.7 %all-reduce.9.cloned.1.call-done = f32[128,896]{1,0:T(8,128)} async-done(((f32[128,896]{1,0:T(8,128)}), f32[128,896]{1,0:T(8,128)}) %all-reduce.9.cloned.1.call-update) | async-done | bytes 458768
  521.1 1.4 fusion.45
  (155 shorter events, 49.5 us)
Async XLA Ops:
  6.5 267.5 %copy-start = (bf16[224,7168]{1,0:T(8,128)(2,1)S(1)}, bf16[224,7168]{1,0:T(8,128)(2,1)}, u32[]{:S(2)}) copy-start(bf16[224,7168]{1,0:T(8,128)(2,1)} %param.28) | copy-start | bytes 9633796
  15.0 75.1 %copy-start.7 = (bf16[16,3584]{1,0:T(8,128)(2,1)S(1)}, bf16[16,3584]{1,0:T(8,128)(2,1)}, u32[]{:S(2)}) copy-start(bf16[16,3584]{1,0:T(8,128)(2,1)} %param.20) | copy-start | bytes 344068
  90.0 19.3 %copy-start.3 = (bf16[16,3584]{1,0:T(8,128)(2,1)}, bf16[16,3584]{1,0:T(8,128)(2,1)S(1)}, u32[]{:S(2)}) copy-start(bf16[16,3584]{1,0:T(8,128)(2,1)S(1)} %dynamic-slice_convert_fusion) | copy-start | bytes 344068
  94.6 12.1 %all-to-all-start = ((bf16[16,8,896]{2,0,1:T(8,128)(2,1)}), bf16[16,8,896]{2,0,1:T(8,128)(2,1)S(1)}, u32[]{:S(2)}, u32[]{:S(2)}) async-start(bf16[16,8,896]{2,0,1:T(8,128)(2,1)} %copy.113), calls=%async_computation | async-start | bytes 458752 | tf_op jit(solution)/shard_map/all_to_all | solution.py:95
  98.5 40.6 %reduce-scatter.2.cloned.1.call-start = ((), (), s32[]{:S(2)}) async-start(), calls=%async_computation.4 | async-start | bytes 442368 | tf_op jit(solution)/shard_map/reduce_scatter | solution.py:97
  109.3 131.8 %all-gather.6.cloned.1.call-start = ((), (), s32[]{:S(2)}) async-start(), calls=%async_computation.6 | async-start | bytes 4456448 | tf_op jit(solution)/shard_map/all_gather | solution.py:15
  123.3 13.2 %copy-start.20 = (f32[4,4]{1,0:T(4,128)S(1)}, f32[4,4]{1,0:T(4,128)}, u32[]{:S(2)}) copy-start(f32[4,4]{1,0:T(4,128)} %add_convert_fusion.2) | copy-start | bytes 196
  123.3 14.0 %copy-start.16 = (s32[768]{0:T(1024)S(1)}, s32[768]{0:T(1024)}, u32[]{:S(2)}) copy-start(s32[768]{0:T(1024)} %iota_bitcast_fusion) | copy-start | bytes 9220
  123.3 14.0 %copy-start.17 = (pred[1,4,6,128]{3,2,1,0:T(8,128)(4,1)S(1)}, pred[1,4,6,128]{3,2,1,0:T(8,128)(4,1)}, u32[]{:S(2)}) copy-start(pred[1,4,6,128]{3,2,1,0:T(8,128)(4,1)} %broadcast_bitcast_fusion.1) | copy-start | bytes 9220
  123.3 14.0 %copy-start.21 = (s32[4]{0:T(128)S(1)}, s32[4]{0:T(128)}, u32[]{:S(2)}) copy-start(s32[4]{0:T(128)} %param.26) | copy-start | bytes 52
  167.4 3.1 copy-start.14
  167.4 3.1 copy-start.15
  170.5 9.2 %slice-start = ((s8[6291456]{0:T(1024)(128)(4,1)}), s8[4194304]{0:T(1024)(128)(4,1)S(1)}, s32[]{:S(2)}) async-start(s8[6291456]{0:T(1024)(128)(4,1)} %bitcast.113), calls=%async_computation.9 | async-start | bytes 8388608
  171.9 6.9 %copy-start.11 = (bf16[4,4,16,112]{3,1,0,2:T(4,128)(2,1)}, bf16[4,4,16,112]{3,1,0,2:T(4,128)(2,1)S(1)}, u32[]{:S(2)}) copy-start(bf16[4,4,16,112]{3,1,0,2:T(4,128)(2,1)S(1)} %get-tuple-element.269) | copy-start | bytes 172036
  171.9 7.8 %slice-start.1 = ((s8[6291456]{0:T(1024)(128)(4,1)}), s8[2097152]{0:T(1024)(128)(4,1)S(1)}, s32[]{:S(2)}) async-start(s8[6291456]{0:T(1024)(128)(4,1)} %bitcast.113), calls=%async_computation.10 | async-start | bytes 4194304
  171.9 7.8 %copy-start.19 = (pred[4,768]{1,0:T(4,128)(4,1)S(1)}, pred[4,768]{1,0:T(4,128)(4,1)}, u32[]{:S(2)}) copy-start(pred[4,768]{1,0:T(4,128)(4,1)} %fusion.54) | copy-start | bytes 9220
  178.8 0.9 copy-start.9
  184.3 55.7 %copy-start.10 = (bf16[16,3584]{1,0:T(8,128)(2,1)S(1)}, bf16[16,3584]{1,0:T(8,128)(2,1)}, u32[]{:S(2)}) copy-start(bf16[16,3584]{1,0:T(8,128)(2,1)} %get-tuple-element.255) | copy-start | bytes 344068
  184.3 172.4 %all-reduce.7.cloned.1.call-start = ((), (), s32[]{:S(2)}) async-start(), calls=%async_computation.5 | async-start | bytes 917504 | tf_op jit(solution)/shard_map/psum | solution.py:169
  211.7 23.1 %copy-start.12 = (f32[64,4,16]{2,1,0:T(4,128)}, f32[64,4,16]{2,1,0:T(4,128)S(1)}, u32[]{:S(2)}) copy-start(f32[64,4,16]{2,1,0:T(4,128)S(1)} %all-gather.1) | copy-start | bytes 49156
  233.6 1.2 copy-start.13
  274.0 1.4 copy-start.18
  274.0 82.7 %copy-start.4 = (bf16[16,3584]{1,0:T(8,128)(2,1)S(1)}, bf16[16,3584]{1,0:T(8,128)(2,1)}, u32[]{:S(2)}) copy-start(bf16[16,3584]{1,0:T(8,128)(2,1)} %copy-done.3) | copy-start | bytes 344068
  274.1 82.7 %copy-start.8 = (bf16[16,3584]{1,0:T(8,128)(2,1)S(1)}, bf16[16,3584]{1,0:T(8,128)(2,1)}, u32[]{:S(2)}) copy-start(bf16[16,3584]{1,0:T(8,128)(2,1)} %param.20) | copy-start | bytes 344068
  275.4 156.4 %all-reduce.11.cloned.1.call-start = ((), (), s32[]{:S(2)}) async-start(), calls=%async_computation.8 | async-start | bytes 1835008 | tf_op jit(solution)/shard_map/psum | solution.py:176
  356.7 12.9 %copy-start.5 = (bf16[896,896]{1,0:T(8,128)(2,1)S(1)}, bf16[896,896]{1,0:T(8,128)(2,1)}, u32[]{:S(2)}) copy-start(bf16[896,896]{1,0:T(8,128)(2,1)} %param.30) | copy-start | bytes 4816900
  358.1 12.9 %copy-start.1 = (bf16[16,7168]{1,0:T(8,128)(2,1)}, bf16[16,7168]{1,0:T(8,128)(2,1)S(1)}, u32[]{:S(2)}) copy-start(bf16[16,7168]{1,0:T(8,128)(2,1)S(1)} %get-tuple-element.249) | copy-start | bytes 688132
  358.1 12.8 %copy-start.6 = (bf16[896,896]{1,0:T(8,128)(2,1)S(1)}, bf16[896,896]{1,0:T(8,128)(2,1)}, u32[]{:S(2)}) copy-start(bf16[896,896]{1,0:T(8,128)(2,1)} %param.31) | copy-start | bytes 4816900
  372.2 148.9 %all-reduce.9.cloned.1.call-start = ((), (), s32[]{:S(2)}) async-start(), calls=%async_computation.7 | async-start | bytes 917504
  433.9 3.2 copy-start.2
  433.9 7.3 %copy-start.22 = (u32[128]{0:T(128)S(1)}, u32[128]{0:T(128)}, u32[]{:S(2)}) copy-start(u32[128]{0:T(128)} %constant.127) | copy-start | bytes 1540
  437.9 10.5 %all-to-all-start.1 = ((bf16[16,8,896]{2,0,1:T(8,128)(2,1)}), bf16[16,8,896]{2,0,1:T(8,128)(2,1)S(1)}, u32[]{:S(2)}, u32[]{:S(2)}) async-start(bf16[16,8,896]{2,0,1:T(8,128)(2,1)} %bitcast.123), calls=%async_computation.2 | async-start | bytes 458752 | tf_op jit(solution)/shard_map/all_to_all | solution.py:173
Sparse Core Ops, SparseCore 0:
  109.4 29.5 reduce-scatter.1
  184.4 48.8 all-gather.5
  275.5 81.1 all-reduce.6
  372.3 59.4 all-reduce.10
  437.3 83.7 all-reduce.8
where the time goes:
time: 532 us; the launch traced here: 529 us
  waiting for transfers between devices  195 us (37%)
  blocking collectives  179 us (34%)
  local copies, waits for them, and re-layouts  66.7 us (13%)
  other arithmetic  40.1 us (8%)
  matrix products  26 us (5%)
  between operations  14.2 us (3%)
  starting transfers between devices  7.46 us (1%)
    psum x1, waiting for transfers between devices, body(): mixed_sum = lax.psum(projected_out, 'seq')  81.3 us
    psum x1, blocking collectives, body(): everywhere = lax.psum(looked, ('seq', 'req'))  74.1 us
    unnamed x6, waiting for transfers between devices  72.8 us
    all_gather x2, blocking collectives, merged_2(): everything = jax.tree.map(lambda part: lax.all_gather(part, axis), array)  44.8 us
    psum x1, waiting for transfers between devices, body(): lax.psum((jnp.dot(second_spread_state, gate_weight, preferred_element_typ...  34.2 us
    all_gather x1, blocking collectives, body(): lax.all_gather(qkv_part.astype(jnp.bfloat16), 'seq', axis=1, tiled=True)  24.2 us
    psum x1, blocking collectives, body(): lax.psum((jnp.dot(second_spread_state, gate_weight, preferred_element_typ...  24.2 us
    dynamic_slice x15, local copies, waits for them, and re-layouts, hop(): return combine(so_far, jax.tree.map(lambda part: part[k], everything))  14.7 us
  transfers between devices with their start and end apart: 7, of which 5 were waited for; matrix products, arithmetic and copies ran while one was open for 10% of the time, Pallas kernels for 0%

commit v1 on v0

--- a/solution.py
+++ b/solution.py
@@ -9,6 +9,24 @@
 NEGATIVE = -1e30
 EPSILON = 1e-05
 ROTARY_BASE = 10000.0
+
+
+def ring_gather(value, axis, dim):
+    ways, here, hop = (lax.axis_size(axis), lax.axis_index(axis), value.shape[dim])
+    lengths = [n * ways if d == dim else n for d, n in enumerate(value.shape)]
+    full = lax.dynamic_update_slice_in_dim(
+        jnp.zeros(lengths, value.dtype), value, here * hop, axis=dim
+    )
+    going_up = going_down = value
+    for far in range(1, ways // 2 + 1):
+        going_up = lax.ppermute(going_up, axis, [(d, (d + 1) % ways) for d in range(ways)])
+        full = lax.dynamic_update_slice_in_dim(full, going_up, (here - far) % ways * hop, axis=dim)
+        if 2 * far < ways:
+            going_down = lax.ppermute(going_down, axis, [(d, (d - 1) % ways) for d in range(ways)])
+            full = lax.dynamic_update_slice_in_dim(
+                full, going_down, (here + far) % ways * hop, axis=dim
+            )
+    return full
 
 
 def merged_2(array, axis, combine):
@@ -100,7 +118,7 @@
         scatter_dimension=0,
         tiled=True,
     )
-    projected = lax.all_gather(qkv_part.astype(jnp.bfloat16), "seq", axis=1, tiled=True)
+    projected = ring_gather(qkv_part.astype(jnp.bfloat16), "seq", 1)
     head_cols = HEADS * HD
     queries = projected[:, :head_cols].reshape(requests, steps_each, HEADS, HD)
     new_keys = projected[:, head_cols : 2 * head_cols].reshape(requests, steps_each, HEADS, HD)

time: 532 us -> 599 us (1.13)
  waiting for transfers between devices: 195 us -> 231 us
  starting transfers between devices: 7.46 us -> 42 us
  local copies, waits for them, and re-layouts: 66.7 us -> 78.7 us
  blocking collectives: 179 us -> 168 us
    ppermute x0 -> x15, starting transfers between devices: none -> 38.5 us  [the longest x7 37 us: ring_gather(): lax.ppermute(going_down, axis, [(d, (d - 1) % ways) for d in range(ways)])]
    reduce_scatter x1, waiting for transfers between devices: 1.11 us -> 27 us  [body(): lax.psum_scatter(jnp.dot(block_rows, query_key_value_weight, preferred_el...]
    all_gather x1 -> x0, blocking collectives: 24.2 us -> none  [body(): lax.all_gather(qkv_part.astype(jnp.bfloat16), 'seq', axis=1, tiled=True)]
    dynamic_update_slice x0 -> x16, local copies, waits for them, and re-layouts: none -> 18.4 us  [the longest x8 9.28 us: ring_gather(): lax.dynamic_update_slice_in_dim(full, going_up, (here - far) % ways * hop...]
    all_to_all x0 -> x1, blocking collectives: none -> 10.8 us  [body(): lax.all_to_all(normed, 'req', split_axis=1, concat_axis=0, tiled=True)]
    ppermute x0 -> x15, waiting for transfers between devices: none -> 10.3 us  [the longest x8 9.37 us: ring_gather(): lax.ppermute(going_up, axis, [(d, (d + 1) % ways) for d in range(ways)])]
  transfers between devices with their start and end apart: 7 -> 21, of which waited for: 5 -> 15; matrix products, arithmetic and copies ran while one was open for 10% -> 10% of each run, Pallas kernels for 0% -> 0%
where the time goes in v1:
time: 599 us; the launch traced here: 595 us
  waiting for transfers between devices  231 us (39%)
  blocking collectives  168 us (28%)
  local copies, waits for them, and re-layouts  78.7 us (13%)
  starting transfers between devices  42 us (7%)
  other arithmetic  35.9 us (6%)
  matrix products  24.7 us (4%)
  between operations  14.4 us (2%)
    psum x1, waiting for transfers between devices, body(): mixed_sum = lax.psum(projected_out, 'seq')  80.5 us
    psum x1, blocking collectives, body(): everywhere = lax.psum(looked, ('seq', 'req'))  74.1 us
    unnamed x6, waiting for transfers between devices  72.8 us
    all_gather x2, blocking collectives, merged_2(): everything = jax.tree.map(lambda part: lax.all_gather(part, axis), array)  47.2 us
    ppermute x7, starting transfers between devices, ring_gather(): lax.ppermute(going_down, axis, [(d, (d - 1) % ways) for d in range(ways)])  37 us
    psum x1, waiting for transfers between devices, body(): lax.psum((jnp.dot(second_spread_state, gate_weight, preferred_element_typ...  34.2 us
    reduce_scatter x1, waiting for transfers between devices, body(): lax.psum_scatter(jnp.dot(block_rows, query_key_value_weight, preferred_el...  27 us
    psum x1, blocking collectives, body(): lax.psum((jnp.dot(second_spread_state, gate_weight, preferred_element_typ...  24.2 us
  transfers between devices with their start and end apart: 21, of which 15 were waited for; matrix products, arithmetic and copies ran while one was open for 10% of the time, Pallas kernels for 0%

profile of v1, /device:TPU:0, one launch (start us, length us, event | category | flops | bytes accessed | tf_op | source)
XLA Modules:
  0.0 594.9 jit_solution(14019605106102674493)
XLA Ops:
  7.4 4.8 gather_fusion
  12.2 2.8 convert_select_fusion
  15.0 74.1 %all-reduce.12 = bf16[128,3584]{1,0:T(8,128)(2,1)} all-reduce(f32[128,3584]{1,0:T(8,128)} %convert_select_fusion), channel_id=1, replica_groups=mesh['seq'=16,'req'=8] {'seq','req'}, use_global_device_ids=true, to_apply=%region_0.1 | all-reduce | flops 458752 | bytes 2752512 | tf_op jit(solution)/shard_map/psum | solution.py:109
  94.1 10.8 %all_to_all.54 = bf16[16,8,896]{2,0,1:T(8,128)(2,1)S(1)} all-to-all(bf16[16,8,896]{2,0,1:T(8,128)(2,1)S(1)} %copy.109), channel_id=1, replica_groups=mesh['seq'=16,'req'=8] {'req'}, dimensions={1} | all-to-all | bytes 458752 | tf_op jit(solution)/shard_map/all_to_all | solution.py:113
  104.9 1.3 fusion.67
  106.7 27.0 %reduce-scatter.2.cloned.1.call-done = f32[16,672]{1,0:T(8,128)} async-done(((f32[128,672]{1,0:T(8,128)}), f32[16,672]{1,0:T(8,128)}) %reduce-scatter.2.cloned.1.call-update) | async-done | bytes 43024 | tf_op jit(solution)/shard_map/reduce_scatter | solution.py:115
  134.5 1.5 collective-permute-start
  136.1 3.9 collective-permute-start.1
  139.9 1.7 collective-permute-done
  142.1 5.4 collective-permute-start.3
  147.5 1.4 collective-permute-done.2
  149.0 5.6 collective-permute-start.5
  154.6 1.6 collective-permute-done.4
  156.2 5.6 collective-permute-start.7
  161.8 1.6 collective-permute-done.6
  164.0 5.4 collective-permute-start.9
  171.1 5.5 collective-permute-start.11
  178.2 5.6 collective-permute-start.13
  185.6 13.1 %reshape.185 = bf16[768,16,224]{2,1,0:T(8,128)(2,1)} reshape(bf16[6,1,128,3584]{3,2,1,0:T(8,128)(2,1)} %param.24) | data formatting | bytes 11010048 | tf_op jit(solution)/shard_map/reshape | solution.py:131
  198.8 13.1 %reshape.186 = bf16[768,16,224]{2,1,0:T(8,128)(2,1)} reshape(bf16[6,1,128,3584]{3,2,1,0:T(8,128)(2,1)} %param.25) | data formatting | bytes 11010048 | tf_op jit(solution)/shard_map/reshape | solution.py:132
  214.1 1.2 dynamic_update_slice.50
  216.5 1.2 dynamic_update_slice.52
  217.7 1.2 dynamic_update_slice.53
  218.9 1.2 dynamic_update_slice.54
  222.1 1.2 dynamic_update_slice.57
  223.3 1.2 dynamic_update_slice.58
  229.3 1.2 dynamic_update_slice.63
  234.5 1.3 subtract_convert_fusion
  235.9 6.8 %select_reduce_fusion = (f32[4,4,16]{1,0,2:T(4,128)S(1)}, f32[4,4,16,768]{3,1,0,2:T(4,128)S(1)}) fusion(pred[4,768]{1,0:T(4,128)(4,1)} %fusion.54, bf16[768,16,224,1]{2,1,0,3:T(8,128)(2,1)} %bitcast.109, bf16[4,4,16,112]{3,1,0,2:T(4,128)(2,1)S(1)} %get-tuple-element.268, bf16[4,4,16,112]{3,1,0,2:T(4,128)(2,1)S(1)} %get-tuple-element.269), kind=kOutput, calls=%fused_computation.25 | convolution fusion | flops 88899328 | bytes 6410240 | tf_op jit(solution)/shard_map/rthd,khd->rthk/dot_general | solution.py:147
  243.6 4.6 fusion.16
  249.6 2.3 fusion.21
  252.7 23.3 %all-gather.1 = f32[64,4,16]{2,1,0:T(4,128)S(1)} all-gather(f32[4,4,16]{2,1,0:T(4,128)S(1)} %copy.114), channel_id=3, replica_groups=mesh['seq'=16,'req'=8] {'seq'}, dimensions={0}, use_global_device_ids=true | all-gather | bytes 17408 | tf_op jit(solution)/shard_map/all_gather | solution.py:33
  276.0 23.9 %all-gather = f32[64,4,16]{2,1,0:T(4,128)S(1)} all-gather(f32[4,4,16]{2,1,0:T(4,128)} %copy.113), channel_id=2, replica_groups=mesh['seq'=16,'req'=8] {'seq'}, dimensions={0}, use_global_device_ids=true | all-gather | bytes 17408 | tf_op jit(solution)/shard_map/all_gather | solution.py:33
  308.6 30.1 %while.19 = (s32[]{:T(128)}, f32[4,4,16]{2,1,0:T(4,128)S(1)}, f32[4,4,16]{2,1,0:T(4,128)S(1)}, f32[4,4,16,224]{3,2,1,0:T(8,128)S(1)}, f32[16,4,4,16]{3,2,1,0:T(4...) while((s32[]{:T(128)}, f32[4,4,16]{2,1,0:T(4,128)S(1)}, ...), condition=%wide.region_8.9_spmd, body=%wide.region_7.8_spmd.sunk | while | flops 173573 | bytes 1157271 | solution.py:39
  340.7 1.3 fusion.68
  342.1 80.5 %all-reduce.7.cloned.1.call-done = f32[16,7168]{1,0:T(8,128)} async-done(((f32[16,7168]{1,0:T(8,128)}), f32[16,7168]{1,0:T(8,128)}) %all-reduce.7.cloned.1.call-update) | async-done | bytes 458768 | tf_op jit(solution)/shard_map/psum | solution.py:187
  422.7 1.3 fusion.24
  424.2 11.4 %all_to_all.55 = bf16[16,8,896]{2,0,1:T(8,128)(2,1)S(1)} all-to-all(bf16[16,8,896]{2,0,1:T(8,128)(2,1)S(1)} %bitcast.117), channel_id=1, replica_groups=mesh['seq'=16,'req'=8] {'req'}, dimensions={1} | all-to-all | bytes 458752 | tf_op jit(solution)/shard_map/all_to_all | solution.py:192
  435.6 1.2 fusion.69
  436.9 1.2 fusion.71
  439.3 24.2 %psum.38 = bf16[128,128]{1,0:T(8,128)(2,1)S(1)} all-reduce(f32[128,128]{1,0:T(8,128)S(1)} %fusion.70), channel_id=1, replica_groups=mesh['seq'=16,'req'=8] {'req'}, use_global_device_ids=true, to_apply=%region_14.15 | all-reduce | flops 16384 | bytes 98304 | tf_op jit(solution)/shard_map/psum | solution.py:194
  463.5 34.2 %all-reduce.11.cloned.1.call-done = (f32[128,896]{1,0:T(8,128)}, f32[128,896]{1,0:T(8,128)}) async-done(((f32[128,896]{1,0:T(8,128)}, f32[128,896]{1,0:T(8,128)}), (f32[128,896]{1,0:T(8,128)}, f32[128,896]{1,0:T(8,128)})) %all-reduce.11.cloned.1.call-update) | async-done | bytes 917520 | tf_op jit(solution)/shard_map/psum | solution.py:194
  497.7 2.1 convolution_add_fusion.1
  499.9 3.2 fusion.19
  503.8 3.4 all-to-all-start.1
  508.5 5.9 all-to-all-done.1
  514.3 72.7 %all-reduce.9.cloned.1.call-done = f32[128,896]{1,0:T(8,128)} async-done(((f32[128,896]{1,0:T(8,128)}), f32[128,896]{1,0:T(8,128)}) %all-reduce.9.cloned.1.call-update) | async-done | bytes 458768
  587.1 1.4 fusion.45
  (220 shorter events, 73.4 us)
Async XLA Ops:
  6.5 334.1 %copy-start = (bf16[224,7168]{1,0:T(8,128)(2,1)S(1)}, bf16[224,7168]{1,0:T(8,128)(2,1)}, u32[]{:S(2)}) copy-start(bf16[224,7168]{1,0:T(8,128)(2,1)} %param.28) | copy-start | bytes 9633796
  6.5 127.2 %reduce-scatter.2.cloned.1.call-start = ((), (), s32[]{:S(2)}) async-start(), calls=%async_computation.4 | async-start | bytes 442368 | tf_op jit(solution)/shard_map/reduce_scatter | solution.py:115
  15.0 75.1 %copy-start.8 = (bf16[16,3584]{1,0:T(8,128)(2,1)S(1)}, bf16[16,3584]{1,0:T(8,128)(2,1)}, u32[]{:S(2)}) copy-start(bf16[16,3584]{1,0:T(8,128)(2,1)} %param.20) | copy-start | bytes 344068
  90.0 16.2 %copy-start.3 = (bf16[16,3584]{1,0:T(8,128)(2,1)}, bf16[16,3584]{1,0:T(8,128)(2,1)S(1)}, u32[]{:S(2)}) copy-start(bf16[16,3584]{1,0:T(8,128)(2,1)S(1)} %dynamic-slice_convert_fusion) | copy-start | bytes 344068
  92.1 14.2 %copy-start.32 = (s32[4]{0:T(128)S(1)}, s32[4]{0:T(128)}, u32[]{:S(2)}) copy-start(s32[4]{0:T(128)} %param.26) | copy-start | bytes 52
  92.1 14.3 %copy-start.31 = (s32[4,48]{1,0:T(4,128)S(1)}, s32[4,48]{1,0:T(4,128)}, u32[]{:S(2)}) copy-start(s32[4,48]{1,0:T(4,128)} %param.27) | copy-start | bytes 2308
  92.9 12.0 %copy-start.7 = (bf16[896,672]{0,1:T(8,128)(2,1)S(1)}, bf16[896,672]{0,1:T(8,128)(2,1)}, u32[]{:S(2)}) copy-start(bf16[896,672]{0,1:T(8,128)(2,1)} %param.23) | copy-start | bytes 3612676
  106.2 201.3 %all-gather.5.cloned.1.call-start = ((), (), s32[]{:S(2)}) async-start(), calls=%async_computation.6 | async-start | bytes 4456448 | tf_op jit(solution)/shard_map/all_gather | solution.py:33
  134.5 64.3 %copy-start.15 = (bf16[16,672]{1,0:T(8,128)(2,1)}, bf16[16,672]{1,0:T(8,128)(2,1)S(1)}, u32[]{:S(2)}) copy-start(bf16[16,672]{1,0:T(8,128)(2,1)S(1)} %convert_element_type.81) | copy-start | bytes 64516
  134.5 7.1 %collective-permute-start = (bf16[16,672]{1,0:T(8,128)(2,1)S(1)}, bf16[16,672]{1,0:T(8,128)(2,1)S(1)}, u32[]{:S(2)}, u32[]{:S(2)}) collective-permute-start(bf16[16,672]{1,0:T(8,128)(2,1)S(1)} %convert_element_type.81), channel_id=1, source_target_pairs={{0,8},{8,16},{16,24},{24,32},{32,40},{40,48},{48,56},{56,64},{64,7... | collective-permute-start | bytes 64520 | tf_op jit(solution)/shard_map/ppermute | solution.py:22
  136.1 6.0 %collective-permute-start.1 = (bf16[16,672]{1,0:T(8,128)(2,1)S(1)}, bf16[16,672]{1,0:T(8,128)(2,1)S(1)}, u32[]{:S(2)}, u32[]{:S(2)}) collective-permute-start(bf16[16,672]{1,0:T(8,128)(2,1)S(1)} %convert_element_type.81), channel_id=1, source_target_pairs={{0,120},{8,0},{16,8},{24,16},{32,24},{40,32},{48,40},{56,48},{64,5... | collective-permute-start | bytes 64520 | tf_op jit(solution)/shard_map/ppermute | solution.py:25
  141.7 57.1 %copy-start.18 = (bf16[16,672]{1,0:T(8,128)(2,1)}, bf16[16,672]{1,0:T(8,128)(2,1)S(1)}, u32[]{:S(2)}) copy-start(bf16[16,672]{1,0:T(8,128)(2,1)S(1)} %collective-permute-done) | copy-start | bytes 64516
  141.7 7.1 %collective-permute-start.2 = (bf16[16,672]{1,0:T(8,128)(2,1)S(1)}, bf16[16,672]{1,0:T(8,128)(2,1)S(1)}, u32[]{:S(2)}, u32[]{:S(2)}) collective-permute-start(bf16[16,672]{1,0:T(8,128)(2,1)S(1)} %collective-permute-done), channel_id=1, source_target_pairs={{0,8},{8,16},{16,24},{24,32},{32,40},{40,48},{48,56},{56,64},{64,7... | collective-permute-start | bytes 64520 | tf_op jit(solution)/shard_map/ppermute | solution.py:22
  142.1 56.7 %copy-start.19 = (bf16[16,672]{1,0:T(8,128)(2,1)}, bf16[16,672]{1,0:T(8,128)(2,1)S(1)}, u32[]{:S(2)}) copy-start(bf16[16,672]{1,0:T(8,128)(2,1)S(1)} %collective-permute-done.1) | copy-start | bytes 64516
  142.1 6.9 %collective-permute-start.3 = (bf16[16,672]{1,0:T(8,128)(2,1)S(1)}, bf16[16,672]{1,0:T(8,128)(2,1)S(1)}, u32[]{:S(2)}, u32[]{:S(2)}) collective-permute-start(bf16[16,672]{1,0:T(8,128)(2,1)S(1)} %collective-permute-done.1), channel_id=1, source_target_pairs={{0,120},{8,0},{16,8},{24,16},{32,24},{40,32},{48,40},{56,48},{64,5... | collective-permute-start | bytes 64520 | tf_op jit(solution)/shard_map/ppermute | solution.py:25
  148.8 50.0 %copy-start.20 = (bf16[16,672]{1,0:T(8,128)(2,1)}, bf16[16,672]{1,0:T(8,128)(2,1)S(1)}, u32[]{:S(2)}) copy-start(bf16[16,672]{1,0:T(8,128)(2,1)S(1)} %collective-permute-done.2) | copy-start | bytes 64516
  148.8 7.3 %collective-permute-start.4 = (bf16[16,672]{1,0:T(8,128)(2,1)S(1)}, bf16[16,672]{1,0:T(8,128)(2,1)S(1)}, u32[]{:S(2)}, u32[]{:S(2)}) collective-permute-start(bf16[16,672]{1,0:T(8,128)(2,1)S(1)} %collective-permute-done.2), channel_id=1, source_target_pairs={{0,8},{8,16},{16,24},{24,32},{32,40},{40,48},{48,56},{56,64},{64,7... | collective-permute-start | bytes 64520 | tf_op jit(solution)/shard_map/ppermute | solution.py:22
  149.0 15.0 %copy-start.21 = (bf16[16,672]{1,0:T(8,128)(2,1)}, bf16[16,672]{1,0:T(8,128)(2,1)S(1)}, u32[]{:S(2)}) copy-start(bf16[16,672]{1,0:T(8,128)(2,1)S(1)} %collective-permute-done.3) | copy-start | bytes 64516
  149.0 7.2 %collective-permute-start.5 = (bf16[16,672]{1,0:T(8,128)(2,1)S(1)}, bf16[16,672]{1,0:T(8,128)(2,1)S(1)}, u32[]{:S(2)}, u32[]{:S(2)}) collective-permute-start(bf16[16,672]{1,0:T(8,128)(2,1)S(1)} %collective-permute-done.3), channel_id=1, source_target_pairs={{0,120},{8,0},{16,8},{24,16},{32,24},{40,32},{48,40},{56,48},{64,5... | collective-permute-start | bytes 64520 | tf_op jit(solution)/shard_map/ppermute | solution.py:25
  156.2 7.8 %copy-start.22 = (bf16[16,672]{1,0:T(8,128)(2,1)}, bf16[16,672]{1,0:T(8,128)(2,1)S(1)}, u32[]{:S(2)}) copy-start(bf16[16,672]{1,0:T(8,128)(2,1)S(1)} %collective-permute-done.4) | copy-start | bytes 64516
  156.2 7.1 %collective-permute-start.6 = (bf16[16,672]{1,0:T(8,128)(2,1)S(1)}, bf16[16,672]{1,0:T(8,128)(2,1)S(1)}, u32[]{:S(2)}, u32[]{:S(2)}) collective-permute-start(bf16[16,672]{1,0:T(8,128)(2,1)S(1)} %collective-permute-done.4), channel_id=1, source_target_pairs={{0,8},{8,16},{16,24},{24,32},{32,40},{40,48},{48,56},{56,64},{64,7... | collective-permute-start | bytes 64520 | tf_op jit(solution)/shard_map/ppermute | solution.py:22
  156.2 13.2 %copy-start.23 = (bf16[16,672]{1,0:T(8,128)(2,1)}, bf16[16,672]{1,0:T(8,128)(2,1)S(1)}, u32[]{:S(2)}) copy-start(bf16[16,672]{1,0:T(8,128)(2,1)S(1)} %collective-permute-done.5) | copy-start | bytes 64516
  156.2 7.8 %collective-permute-start.7 = (bf16[16,672]{1,0:T(8,128)(2,1)S(1)}, bf16[16,672]{1,0:T(8,128)(2,1)S(1)}, u32[]{:S(2)}, u32[]{:S(2)}) collective-permute-start(bf16[16,672]{1,0:T(8,128)(2,1)S(1)} %collective-permute-done.5), channel_id=1, source_target_pairs={{0,120},{8,0},{16,8},{24,16},{32,24},{40,32},{48,40},{56,48},{64,5... | collective-permute-start | bytes 64520 | tf_op jit(solution)/shard_map/ppermute | solution.py:25
  163.3 7.2 %copy-start.24 = (bf16[16,672]{1,0:T(8,128)(2,1)}, bf16[16,672]{1,0:T(8,128)(2,1)S(1)}, u32[]{:S(2)}) copy-start(bf16[16,672]{1,0:T(8,128)(2,1)S(1)} %collective-permute-done.6) | copy-start | bytes 64516
  163.3 7.1 %collective-permute-start.8 = (bf16[16,672]{1,0:T(8,128)(2,1)S(1)}, bf16[16,672]{1,0:T(8,128)(2,1)S(1)}, u32[]{:S(2)}, u32[]{:S(2)}) collective-permute-start(bf16[16,672]{1,0:T(8,128)(2,1)S(1)} %collective-permute-done.6), channel_id=1, source_target_pairs={{0,8},{8,16},{16,24},{24,32},{32,40},{40,48},{48,56},{56,64},{64,7... | collective-permute-start | bytes 64520 | tf_op jit(solution)/shard_map/ppermute | solution.py:22
  164.0 6.9 %collective-permute-start.9 = (bf16[16,672]{1,0:T(8,128)(2,1)S(1)}, bf16[16,672]{1,0:T(8,128)(2,1)S(1)}, u32[]{:S(2)}, u32[]{:S(2)}) collective-permute-start(bf16[16,672]{1,0:T(8,128)(2,1)S(1)} %collective-permute-done.7), channel_id=1, source_target_pairs={{0,120},{8,0},{16,8},{24,16},{32,24},{40,32},{48,40},{56,48},{64,5... | collective-permute-start | bytes 64520 | tf_op jit(solution)/shard_map/ppermute | solution.py:25
  170.5 7.1 %collective-permute-start.10 = (bf16[16,672]{1,0:T(8,128)(2,1)S(1)}, bf16[16,672]{1,0:T(8,128)(2,1)S(1)}, u32[]{:S(2)}, u32[]{:S(2)}) collective-permute-start(bf16[16,672]{1,0:T(8,128)(2,1)S(1)} %collective-permute-done.8), channel_id=1, source_target_pairs={{0,8},{8,16},{16,24},{24,32},{32,40},{40,48},{48,56},{56,64},{64,7... | collective-permute-start | bytes 64520 | tf_op jit(solution)/shard_map/ppermute | solution.py:22
  171.1 6.5 %copy-start.27 = (bf16[16,672]{1,0:T(8,128)(2,1)}, bf16[16,672]{1,0:T(8,128)(2,1)S(1)}, u32[]{:S(2)}) copy-start(bf16[16,672]{1,0:T(8,128)(2,1)S(1)} %collective-permute-done.9) | copy-start | bytes 64516
  171.1 7.0 %collective-permute-start.11 = (bf16[16,672]{1,0:T(8,128)(2,1)S(1)}, bf16[16,672]{1,0:T(8,128)(2,1)}, u32[]{:S(2)}, u32[]{:S(2)}) collective-permute-start(bf16[16,672]{1,0:T(8,128)(2,1)S(1)} %collective-permute-done.9), channel_id=1, source_target_pairs={{0,120},{8,0},{16,8},{24,16},{32,24},{40,32},{48,40},{56,48},{64,5... | collective-permute-start | bytes 64520 | tf_op jit(solution)/shard_map/ppermute | solution.py:25
  177.6 7.3 %collective-permute-start.12 = (bf16[16,672]{1,0:T(8,128)(2,1)S(1)}, bf16[16,672]{1,0:T(8,128)(2,1)}, u32[]{:S(2)}, u32[]{:S(2)}) collective-permute-start(bf16[16,672]{1,0:T(8,128)(2,1)S(1)} %collective-permute-done.10), channel_id=1, source_target_pairs={{0,8},{8,16},{16,24},{24,32},{32,40},{40,48},{48,56},{56,64},{64,7... | collective-permute-start | bytes 64520 | tf_op jit(solution)/shard_map/ppermute | solution.py:22
  178.2 49.8 %collective-permute-start.13 = (bf16[16,672]{1,0:T(8,128)(2,1)}, bf16[16,672]{1,0:T(8,128)(2,1)}, u32[]{:S(2)}, u32[]{:S(2)}) collective-permute-start(bf16[16,672]{1,0:T(8,128)(2,1)} %collective-permute-done.11), channel_id=1, source_target_pairs={{0,120},{8,0},{16,8},{24,16},{32,24},{40,32},{48,40},{56,48},{64,5... | collective-permute-start | bytes 64520 | tf_op jit(solution)/shard_map/ppermute | solution.py:25
  184.9 44.4 %collective-permute-start.14 = (bf16[16,672]{1,0:T(8,128)(2,1)}, bf16[16,672]{1,0:T(8,128)(2,1)}, u32[]{:S(2)}, u32[]{:S(2)}) collective-permute-start(bf16[16,672]{1,0:T(8,128)(2,1)} %collective-permute-done.12), channel_id=1, source_target_pairs={{0,8},{8,16},{16,24},{24,32},{32,40},{40,48},{48,56},{56,64},{64,7... | collective-permute-start | bytes 64520 | tf_op jit(solution)/shard_map/ppermute | solution.py:22
  234.5 9.1 %slice-start = ((s8[6291456]{0:T(1024)(128)(4,1)}), s8[4194304]{0:T(1024)(128)(4,1)S(1)}, s32[]{:S(2)}) async-start(s8[6291456]{0:T(1024)(128)(4,1)} %bitcast.106), calls=%async_computation.9 | async-start | bytes 8388608
  235.9 6.9 %copy-start.12 = (bf16[4,4,16,112]{3,1,0,2:T(4,128)(2,1)}, bf16[4,4,16,112]{3,1,0,2:T(4,128)(2,1)S(1)}, u32[]{:S(2)}) copy-start(bf16[4,4,16,112]{3,1,0,2:T(4,128)(2,1)S(1)} %get-tuple-element.269) | copy-start | bytes 172036
  235.9 7.8 %slice-start.1 = ((s8[6291456]{0:T(1024)(128)(4,1)}), s8[2097152]{0:T(1024)(128)(4,1)S(1)}, s32[]{:S(2)}) async-start(s8[6291456]{0:T(1024)(128)(4,1)} %bitcast.106), calls=%async_computation.10 | async-start | bytes 4194304
  235.9 7.8 %copy-start.30 = (pred[4,768]{1,0:T(4,128)(4,1)S(1)}, pred[4,768]{1,0:T(4,128)(4,1)}, u32[]{:S(2)}) copy-start(pred[4,768]{1,0:T(4,128)(4,1)} %fusion.54) | copy-start | bytes 9220
  248.2 58.2 %copy-start.11 = (bf16[16,3584]{1,0:T(8,128)(2,1)S(1)}, bf16[16,3584]{1,0:T(8,128)(2,1)}, u32[]{:S(2)}) copy-start(bf16[16,3584]{1,0:T(8,128)(2,1)} %get-tuple-element.255) | copy-start | bytes 344068
  248.2 174.5 %all-reduce.7.cloned.1.call-start = ((), (), s32[]{:S(2)}) async-start(), calls=%async_computation.5 | async-start | bytes 917504 | tf_op jit(solution)/shard_map/psum | solution.py:187
  276.0 25.1 %copy-start.13 = (f32[64,4,16]{2,1,0:T(4,128)}, f32[64,4,16]{2,1,0:T(4,128)S(1)}, u32[]{:S(2)}) copy-start(f32[64,4,16]{2,1,0:T(4,128)S(1)} %all-gather.1) | copy-start | bytes 49156
  340.7 82.0 %copy-start.4 = (bf16[16,3584]{1,0:T(8,128)(2,1)S(1)}, bf16[16,3584]{1,0:T(8,128)(2,1)}, u32[]{:S(2)}) copy-start(bf16[16,3584]{1,0:T(8,128)(2,1)} %copy-done.3) | copy-start | bytes 344068
  340.7 82.0 %copy-start.9 = (bf16[16,3584]{1,0:T(8,128)(2,1)S(1)}, bf16[16,3584]{1,0:T(8,128)(2,1)}, u32[]{:S(2)}) copy-start(bf16[16,3584]{1,0:T(8,128)(2,1)} %param.20) | copy-start | bytes 344068
  342.1 155.7 %all-reduce.11.cloned.1.call-start = ((), (), s32[]{:S(2)}) async-start(), calls=%async_computation.8 | async-start | bytes 1835008 | tf_op jit(solution)/shard_map/psum | solution.py:194
  422.7 12.9 %copy-start.5 = (bf16[896,896]{1,0:T(8,128)(2,1)S(1)}, bf16[896,896]{1,0:T(8,128)(2,1)}, u32[]{:S(2)}) copy-start(bf16[896,896]{1,0:T(8,128)(2,1)} %param.30) | copy-start | bytes 4816900
  424.0 12.9 %copy-start.1 = (bf16[16,7168]{1,0:T(8,128)(2,1)}, bf16[16,7168]{1,0:T(8,128)(2,1)S(1)}, u32[]{:S(2)}) copy-start(bf16[16,7168]{1,0:T(8,128)(2,1)S(1)} %get-tuple-element.249) | copy-start | bytes 688132
  424.0 12.8 %copy-start.6 = (bf16[896,896]{1,0:T(8,128)(2,1)S(1)}, bf16[896,896]{1,0:T(8,128)(2,1)}, u32[]{:S(2)}) copy-start(bf16[896,896]{1,0:T(8,128)(2,1)} %param.31) | copy-start | bytes 4816900
  438.1 148.9 %all-reduce.9.cloned.1.call-start = ((), (), s32[]{:S(2)}) async-start(), calls=%async_computation.7 | async-start | bytes 917504
  499.9 7.4 %copy-start.33 = (u32[128]{0:T(128)S(1)}, u32[128]{0:T(128)}, u32[]{:S(2)}) copy-start(u32[128]{0:T(128)} %constant.223) | copy-start | bytes 1540
  503.8 10.5 %all-to-all-start.1 = ((bf16[16,8,896]{2,0,1:T(8,128)(2,1)}), bf16[16,8,896]{2,0,1:T(8,128)(2,1)S(1)}, u32[]{:S(2)}, u32[]{:S(2)}) async-start(bf16[16,8,896]{2,0,1:T(8,128)(2,1)} %bitcast.115), calls=%async_computation.2 | async-start | bytes 458752 | tf_op jit(solution)/shard_map/all_to_all | solution.py:191
  (9 other events, 20.7 us)
Sparse Core Ops, SparseCore 0:
  106.3 27.3 reduce-scatter.1
  248.3 50.6 all-gather.4
  342.2 80.4 all-reduce.6
  438.3 59.4 all-reduce.10
  503.2 83.7 all-reduce.8
